TPU v7x, 32 devices: a whole 2x2x4 slice. The times are simulated.
32 devices in a mesh: rep: 8 (over z, y), fsdp: 2 (over x), ctx: 2 (over core).
Axes of the slice: x: 2, y: 2, z: 4, core: 2. Of those that a mesh axis runs over, the one named last changes fastest.
Arguments:
- tokens: bfloat16 [32, 1024, 1280], P(('rep', 'fsdp'), 'ctx'), may hold values from -6 to 6
- prefixes: int32 [32], P(('rep', 'fsdp')), may hold values from 102 to 512, as said below
- query_weight: bfloat16 [1280, 1280], P(('fsdp', 'ctx')), may hold values from -0.15625 to 0.15625
- key_weight: bfloat16 [1280, 1280], P(('fsdp', 'ctx')), may hold values from -0.15625 to 0.15625
- value_weight: bfloat16 [1280, 1280], P(('fsdp', 'ctx')), may hold values from -0.15625 to 0.15625
- output_weight: bfloat16 [1280, 1280], P(('fsdp', 'ctx')), may hold values from -2 to 2
- up_weight: bfloat16 [1280, 1280], P(('fsdp', 'ctx')), may hold values from -0.15625 to 0.15625
- up_bias: float32 [1280], replicated, may hold values from -3 to 3
- down_weight: bfloat16 [1280, 1280], P(('fsdp', 'ctx')), may hold values from -0.15625 to 0.15625
- down_bias: float32 [1280], replicated, may hold values from -3 to 3
- attn_gain: float32 [1280], replicated, may hold values from 0.5 to 1.5
- mlp_gain: float32 [1280], replicated, may hold values from 0.5 to 1.5
- query_scale: float32 [80], replicated, may hold values from -2.5 to 2.5
- cotangent: bfloat16 [32, 1024, 1280], P(('rep', 'fsdp'), 'ctx'), may hold values from -6 to 6
Outputs:
- mixed: bfloat16 [32, 1024, 1280], P(('rep', 'fsdp'), 'ctx')
- tokens_grad: bfloat16 [32, 1024, 1280], P(('rep', 'fsdp'), 'ctx')
- query_grad: float32 [1280, 1280], P(('fsdp', 'ctx'))
- key_grad: float32 [1280, 1280], P(('fsdp', 'ctx'))
- value_grad: float32 [1280, 1280], P(('fsdp', 'ctx'))
- output_grad: float32 [1280, 1280], P(('fsdp', 'ctx'))
- up_grad: float32 [1280, 1280], P(('fsdp', 'ctx'))
- upbias_grad: float32 [1280], replicated
- down_grad: float32 [1280, 1280], P(('fsdp', 'ctx'))
- downbias_grad: float32 [1280], replicated
- attngain_grad: float32 [1280], replicated
- mlpgain_grad: float32 [1280], replicated
- scale_grad: float32 [80], replicated
Inputs may be any that keep to these rules, and one draw needn't show every extreme that they name: `prefixes`: at least one sequence has 1024 // 10 and one has 1024 // 2.
All inputs are finite; a program needn't handle non-finite values.
Results may differ from a plain program's by a relative error of at most 0.02.
Values may be sent and summed in bfloat16 or wider, within the bound.
No kernel may reach another device: no remote copies, remote signals or barrier semaphores. Data moves between devices by JAX's collectives and lax.ppermute only.
A program may use at most 384 MiB of HBM per device.

v0:
```python
import jax
import jax.numpy as jnp
from jax import lax
from jax.sharding import PartitionSpec as P

HD = 80
epsilon = 1e-06
softplus_gain = 1.442695041
masked_value = -1e30


def norm_factor(values):
    return lax.rsqrt(jnp.mean(values * values, axis=-1, keepdims=True) + epsilon)


def norm_back(upstream, values, factor, gain_vec):
    scaled = upstream * gain_vec
    row_inner = jnp.mean(scaled * values, axis=-1, keepdims=True)
    return factor * scaled - values * factor**3 * row_inner


def allowed_mask(offset, local_rows, length, prefix):
    row_index = offset + jnp.arange(local_rows, dtype=jnp.int32)[:, None]
    col_index = jnp.arange(length, dtype=jnp.int32)[None, :]
    return (col_index <= row_index) | (col_index < prefix)


def masked_scores(queries, keys, allowed):
    scores = jnp.einsum("qhe,khe->hqk", queries, keys, preferred_element_type=jnp.float32)
    return jnp.where(allowed[None], scores, masked_value)


def shards(
    tokens,
    prefixes,
    query_weight,
    key_weight,
    value_weight,
    output_weight,
    up_weight,
    up_bias,
    down_weight,
    down_bias,
    attn_gain,
    mlp_gain,
    query_scale,
    cotangent,
):
    seq_count, local_rows, model_width = tokens.shape
    head_count = model_width // HD
    position_index = lax.axis_index("ctx")
    offset = position_index * local_rows
    full_query, full_key, full_value, full_output, full_up, full_down = (
        lax.all_gather(query_weight, ("fsdp", "ctx"), axis=0, tiled=True),
        lax.all_gather(key_weight, ("fsdp", "ctx"), axis=0, tiled=True),
        lax.all_gather(value_weight, ("fsdp", "ctx"), axis=0, tiled=True),
        lax.all_gather(output_weight, ("fsdp", "ctx"), axis=0, tiled=True),
        lax.all_gather(up_weight, ("fsdp", "ctx"), axis=0, tiled=True),
        lax.all_gather(down_weight, ("fsdp", "ctx"), axis=0, tiled=True),
    )
    rows_in = tokens.reshape(seq_count * local_rows, model_width).astype(jnp.float32)
    factor_one = norm_factor(rows_in)
    normed = (rows_in * factor_one * attn_gain).astype(jnp.bfloat16)
    scale_soft = jax.nn.softplus(query_scale) * (softplus_gain * HD ** (-0.5))
    query_raw = jnp.dot(normed, full_query, preferred_element_type=jnp.float32).reshape(
        seq_count, local_rows, head_count, HD
    )
    queries = (query_raw * scale_soft).astype(jnp.bfloat16)
    key_local = (
        jnp.dot(normed, full_key, preferred_element_type=jnp.float32)
        .astype(jnp.bfloat16)
        .reshape(seq_count, local_rows, model_width)
    )
    value_local = (
        jnp.dot(normed, full_value, preferred_element_type=jnp.float32)
        .astype(jnp.bfloat16)
        .reshape(seq_count, local_rows, model_width)
    )
    key_all, value_all = (
        lax.all_gather(key_local, "ctx", axis=1, tiled=True),
        lax.all_gather(value_local, "ctx", axis=1, tiled=True),
    )
    length = key_all.shape[1]

    def forward_one(members):
        queries_seq, keys_seq, values_seq, prefix = members
        allowed = allowed_mask(offset, local_rows, length, prefix)
        scores = masked_scores(queries_seq, keys_seq.reshape(length, head_count, HD), allowed)
        row_max = jnp.max(scores, axis=-1, keepdims=True)
        weights = jnp.exp(scores - row_max)
        row_total = jnp.sum(weights, axis=-1, keepdims=True)
        probability = (weights / row_total).astype(jnp.bfloat16)
        context = jnp.einsum(
            "hqk,khe->qhe",
            probability,
            values_seq.reshape(length, head_count, HD),
            preferred_element_type=jnp.float32,
        )
        return (context, row_max + jnp.log(row_total))

    context, logsum = lax.map(forward_one, (queries, key_all, value_all, prefixes))
    attended = context.reshape(seq_count * local_rows, model_width).astype(jnp.bfloat16)
    middle = rows_in + jnp.dot(attended, full_output, preferred_element_type=jnp.float32)
    factor_two = norm_factor(middle)
    normed_two = (middle * factor_two * mlp_gain).astype(jnp.bfloat16)
    before = jnp.dot(normed_two, full_up, preferred_element_type=jnp.float32) + up_bias
    hidden = jax.nn.silu(before).astype(jnp.bfloat16)
    mixed_rows = middle + jnp.dot(hidden, full_down, preferred_element_type=jnp.float32) + down_bias
    mixed_out = mixed_rows.astype(jnp.bfloat16).reshape(seq_count, local_rows, model_width)
    key_back, value_back = (key_all, value_all)
    back_query, back_key, back_value, back_output, back_up, back_down = (
        lax.all_gather(query_weight, ("fsdp", "ctx"), axis=0, tiled=True),
        lax.all_gather(key_weight, ("fsdp", "ctx"), axis=0, tiled=True),
        lax.all_gather(value_weight, ("fsdp", "ctx"), axis=0, tiled=True),
        lax.all_gather(output_weight, ("fsdp", "ctx"), axis=0, tiled=True),
        lax.all_gather(up_weight, ("fsdp", "ctx"), axis=0, tiled=True),
        lax.all_gather(down_weight, ("fsdp", "ctx"), axis=0, tiled=True),
    )
    key_back, value_back = (
        lax.all_gather(key_local, "ctx", axis=1, tiled=True),
        lax.all_gather(value_local, "ctx", axis=1, tiled=True),
    )
    upstream = cotangent.reshape(seq_count * local_rows, model_width)
    upstream_wide = upstream.astype(jnp.float32)
    down_part = jnp.einsum("nf,nd->fd", hidden, upstream, preferred_element_type=jnp.float32)
    downbias_part = jnp.sum(upstream_wide, axis=0)
    hidden_grad = jnp.einsum("nd,fd->nf", upstream, back_down, preferred_element_type=jnp.float32)
    gate_sig = jax.nn.sigmoid(before)
    before_grad = (hidden_grad * gate_sig * (1.0 + before * (1.0 - gate_sig))).astype(jnp.bfloat16)
    up_part = jnp.einsum("nd,nf->df", normed_two, before_grad, preferred_element_type=jnp.float32)
    upbias_part = jnp.sum(before_grad.astype(jnp.float32), axis=0)
    normed_grad = jnp.einsum("nf,df->nd", before_grad, back_up, preferred_element_type=jnp.float32)
    mlpgain_part = jnp.sum(normed_grad * middle * factor_two, axis=0)
    middle_grad = upstream_wide + norm_back(normed_grad, middle, factor_two, mlp_gain)
    middle_low = middle_grad.astype(jnp.bfloat16)
    output_part = jnp.einsum("nd,ne->de", attended, middle_low, preferred_element_type=jnp.float32)
    context_grad = jnp.einsum(
        "ne,de->nd", middle_low, back_output, preferred_element_type=jnp.float32
    )
    context_grad = context_grad.astype(jnp.bfloat16).reshape(seq_count, local_rows, head_count, HD)

    def backward_one(members):
        queries_seq, keys_seq, values_seq, grad_seq, logsum_seq, prefix = members
        keys_heads = keys_seq.reshape(length, head_count, HD)
        values_heads = values_seq.reshape(length, head_count, HD)
        allowed = allowed_mask(offset, local_rows, length, prefix)
        scores = masked_scores(queries_seq, keys_heads, allowed)
        exact_prob = jnp.exp(scores - logsum_seq)
        probability = exact_prob.astype(jnp.bfloat16)
        prob_grad = jnp.einsum(
            "qhe,khe->hqk", grad_seq, values_heads, preferred_element_type=jnp.float32
        )
        row_inner = jnp.sum(prob_grad * exact_prob, axis=-1, keepdims=True)
        score_grad = (exact_prob * (prob_grad - row_inner)).astype(jnp.bfloat16)
        query_part = jnp.einsum(
            "hqk,khe->qhe", score_grad, keys_heads, preferred_element_type=jnp.float32
        )
        key_term = jnp.einsum(
            "hqk,qhe->khe", score_grad, queries_seq, preferred_element_type=jnp.float32
        )
        value_term = jnp.einsum(
            "hqk,qhe->khe", probability, grad_seq, preferred_element_type=jnp.float32
        )
        return (
            query_part,
            key_term.reshape(length, model_width),
            value_term.reshape(length, model_width),
        )

    query_seqgrad, key_partial, value_partial = lax.map(
        backward_one, (queries, key_back, value_back, context_grad, logsum, prefixes)
    )
    key_summed, value_summed = (
        lax.psum_scatter(key_partial, "ctx", scatter_dimension=1, tiled=True),
        lax.psum_scatter(value_partial, "ctx", scatter_dimension=1, tiled=True),
    )
    key_low = key_summed.astype(jnp.bfloat16).reshape(seq_count * local_rows, model_width)
    value_low = value_summed.astype(jnp.bfloat16).reshape(seq_count * local_rows, model_width)
    scaled_low = query_seqgrad.astype(jnp.bfloat16)
    query_low = (
        (scaled_low * scale_soft).astype(jnp.bfloat16).reshape(seq_count * local_rows, model_width)
    )
    scale_part = jnp.sum(scaled_low * query_raw, axis=(0, 1, 2))
    scale_part = scale_part * jax.nn.sigmoid(query_scale) * (softplus_gain * HD ** (-0.5))
    query_part = jnp.einsum("nd,ne->de", normed, query_low, preferred_element_type=jnp.float32)
    key_part = jnp.einsum("nd,ne->de", normed, key_low, preferred_element_type=jnp.float32)
    value_part = jnp.einsum("nd,ne->de", normed, value_low, preferred_element_type=jnp.float32)
    normed_grad_one = jnp.einsum(
        "ne,de->nd", query_low, back_query, preferred_element_type=jnp.float32
    )
    normed_grad_one = normed_grad_one + jnp.einsum(
        "ne,de->nd", key_low, back_key, preferred_element_type=jnp.float32
    )
    normed_grad_one = normed_grad_one + jnp.einsum(
        "ne,de->nd", value_low, back_value, preferred_element_type=jnp.float32
    )
    attngain_part = jnp.sum(normed_grad_one * rows_in * factor_one, axis=0)
    tokens_grad = middle_grad + norm_back(normed_grad_one, rows_in, factor_one, attn_gain)
    tokens_grad = tokens_grad.astype(jnp.bfloat16).reshape(seq_count, local_rows, model_width)
    query_shard, key_shard, value_shard, output_shard, up_shard, down_shard = (
        lax.psum_scatter(
            query_part.astype(jnp.bfloat16), ("fsdp", "ctx"), scatter_dimension=0, tiled=True
        ).astype(jnp.float32),
        lax.psum_scatter(
            key_part.astype(jnp.bfloat16), ("fsdp", "ctx"), scatter_dimension=0, tiled=True
        ).astype(jnp.float32),
        lax.psum_scatter(
            value_part.astype(jnp.bfloat16), ("fsdp", "ctx"), scatter_dimension=0, tiled=True
        ).astype(jnp.float32),
        lax.psum_scatter(
            output_part.astype(jnp.bfloat16), ("fsdp", "ctx"), scatter_dimension=0, tiled=True
        ).astype(jnp.float32),
        lax.psum_scatter(
            up_part.astype(jnp.bfloat16), ("fsdp", "ctx"), scatter_dimension=0, tiled=True
        ).astype(jnp.float32),
        lax.psum_scatter(
            down_part.astype(jnp.bfloat16), ("fsdp", "ctx"), scatter_dimension=0, tiled=True
        ).astype(jnp.float32),
    )
    query_total, key_total, value_total, output_total, up_total, down_total = (
        lax.psum(query_shard.astype(jnp.bfloat16), "rep").astype(jnp.float32),
        lax.psum(key_shard.astype(jnp.bfloat16), "rep").astype(jnp.float32),
        lax.psum(value_shard.astype(jnp.bfloat16), "rep").astype(jnp.float32),
        lax.psum(output_shard.astype(jnp.bfloat16), "rep").astype(jnp.float32),
        lax.psum(up_shard.astype(jnp.bfloat16), "rep").astype(jnp.float32),
        lax.psum(down_shard.astype(jnp.bfloat16), "rep").astype(jnp.float32),
    )
    upbias_total, downbias_total, attngain_total, mlpgain_total, scale_total = lax.psum(
        (upbias_part, downbias_part, attngain_part, mlpgain_part, scale_part),
        ("rep", "fsdp", "ctx"),
    )
    return (
        mixed_out,
        tokens_grad,
        query_total,
        key_total,
        value_total,
        output_total,
        up_total,
        upbias_total,
        down_total,
        downbias_total,
        attngain_total,
        mlpgain_total,
        scale_total,
    )


def solution(mesh):
    return jax.shard_map(
        shards,
        mesh=mesh,
        in_specs=(
            P(("rep", "fsdp"), "ctx", None),
            P(("rep", "fsdp")),
            P(("fsdp", "ctx"), None),
            P(("fsdp", "ctx"), None),
            P(("fsdp", "ctx"), None),
            P(("fsdp", "ctx"), None),
            P(("fsdp", "ctx"), None),
            P(),
            P(("fsdp", "ctx"), None),
            P(),
            P(),
            P(),
            P(),
            P(("rep", "fsdp"), "ctx", None),
        ),
        out_specs=(
            P(("rep", "fsdp"), "ctx", None),
            P(("rep", "fsdp"), "ctx", None),
            P(("fsdp", "ctx"), None),
            P(("fsdp", "ctx"), None),
            P(("fsdp", "ctx"), None),
            P(("fsdp", "ctx"), None),
            P(("fsdp", "ctx"), None),
            P(),
            P(("fsdp", "ctx"), None),
            P(),
            P(),
            P(),
            P(),
        ),
        check_vma=False,
    )
```

profile of v0, /device:TPU:0, one launch (start us, length us, event | category | flops | bytes accessed | tf_op | source)
XLA Modules:
  0.0 1070.1 jit_solution(11149948379400811405)
XLA Ops:
  15.3 26.3 %all-gather.15.cloned.1.call-done = bf16[1280,1280]{1,0:T(8,128)(2,1)} async-done(((bf16[320,1280]{1,0:T(8,128)(2,1)}), bf16[1280,1280]{1,0:T(8,128)(2,1)}) %all-gather.15.cloned.1.call-update) | async-done | bytes 3276816 | tf_op jit(solution)/shard_map/all_gather | solution.py:55
  41.6 7.8 convolution_convert_fusion.5
  49.3 4.5 copy.37
  53.9 18.5 %all-gather.9.cloned.1.call-done = bf16[1280,1280]{1,0:T(8,128)(2,1)} async-done(((bf16[320,1280]{1,0:T(8,128)(2,1)}), bf16[1280,1280]{1,0:T(8,128)(2,1)}) %all-gather.9.cloned.1.call-update) | async-done | bytes 3276816 | tf_op jit(solution)/shard_map/all_gather | solution.py:56
  72.4 7.8 convolution_convert_fusion.6
  80.2 4.5 copy.35
  89.3 14.0 %all-gather.13.cloned.1.call-done = bf16[1280,1280]{1,0:T(8,128)(2,1)} async-done(((bf16[320,1280]{1,0:T(8,128)(2,1)}), bf16[1280,1280]{1,0:T(8,128)(2,1)}) %all-gather.13.cloned.1.call-update) | async-done | bytes 3276816 | tf_op jit(solution)/shard_map/all_gather | solution.py:54
  103.3 5.6 copy.36
  108.9 9.2 multiply_convert_fusion.4
  119.9 18.4 %all-gather.11.cloned.1.call-done = bf16[2,1024,1280]{1,2,0:T(8,128)(2,1)} async-done(((bf16[2,512,1280]{1,2,0:T(8,128)(2,1)}), bf16[2,1024,1280]{1,2,0:T(8,128)(2,1)}) %all-gather.11.cloned.1.call-update) | async-done | bytes 5242896 | tf_op jit(solution)/shard_map/all_gather | solution.py:81
  140.1 103.8 %while.26 = (s32[]{:T(128)}, bf16[2,512,16,80]{1,3,2,0:T(8,128)(2,1)}, f32[2,16,512,1]{2,1,3,0:T(8,128)S(1)}, bf16[2,1024,1280]{1,2,0:T(8,128)(2,1)}, s32[]{:T(1...) while((s32[]{:T(128)}, ...), condition=%wide.region_4.5_spmd, body=%wide.region_1.4_spmd.sunk | while | flops 2760893952 | bytes 154147024 | solution.py:101
  141.7 4.6 constant_dynamic-slice_fusion.7
  146.4 13.5 %select_reduce_fusion.2 = (f32[16,512]{1,0:T(8,128)S(1)}, f32[16,512,1024]{2,1,0:T(8,128)}) fusion(pred[512,1024]{1,0:T(8,128)(4,1)S(1)} %fusion.112, bf16[1024,16,80]{0,2,1:T(8,128)(2,1)S(1)} %bitcast.193, bf16[2,512,16,80]{1,3,2,0:T(8,128)(2,1)S(1)} %get-tuple-element.373, s32[]{:T(128)S(6)} %copy.79), kind=kOutput, calls=%fused_computation.2.clone.1 | convolution fusion | flops 1358946304 | bytes 38043652 | tf_op jit(solution)/shard_map/while/body/eval_jaxpr/qhe,khe->hqk/dot_general | solution.py:29
  159.9 15.4 %fusion.113 = f32[16,512]{1,0:T(8,128)S(1)} fusion(f32[16,512,1024]{2,1,0:T(8,128)} %get-tuple-element.332, f32[16,512]{1,0:T(8,128)S(1)} %get-tuple-element.333, pred[512,1024]{1,0:T(8,128)(4,1)S(1)} %fusion.112), kind=kLoop, calls=%fused_computation.3.clone.1 | loop fusion | flops 25157632 | bytes 34144256 | tf_op jit(solution)/shard_map/while/body/eval_jaxpr/reduce_sum | solution.py:91
  175.3 15.2 %bitcast_dynamic-update-slice_fusion.6 = bf16[2,512,16,80]{1,3,2,0:T(8,128)(2,1)S(1)} fusion(bf16[2,512,16,80]{1,3,2,0:T(8,128)(2,1)S(1)} %copy-done.8, s32[]{:T(128)S(6)} %copy.79, bf16[1024,16,80]{0,2,1:T(8,128)(2,1)S(1)} %bitcast.196, f32[16,512,1024]{2,1,0:T(8,128)} %get-tuple-element.332, f32[16,512]{1,0:T(8,128)S(1)} %fusion.113, ...), kind=kOutput, calls=%fused_computation.5.clone.1 | convolution fusion | flops 1375731712 | bytes 39387140 | tf_op jit(solution)/shard_map/while/body/eval_jaxpr/hqk,khe->qhe/dot_general | solution.py:93
  193.6 4.6 constant_dynamic-slice_fusion.7
  198.3 14.3 %select_reduce_fusion.2 = (f32[16,512]{1,0:T(8,128)S(1)}, f32[16,512,1024]{2,1,0:T(8,128)}) fusion(pred[512,1024]{1,0:T(8,128)(4,1)S(1)} %fusion.112, bf16[1024,16,80]{0,2,1:T(8,128)(2,1)S(1)} %bitcast.193, bf16[2,512,16,80]{1,3,2,0:T(8,128)(2,1)S(1)} %get-tuple-element.373, s32[]{:T(128)S(6)} %copy.79), kind=kOutput, calls=%fused_computation.2.clone.1 | convolution fusion | flops 1358946304 | bytes 38043652 | tf_op jit(solution)/shard_map/while/body/eval_jaxpr/qhe,khe->hqk/dot_general | solution.py:29
  212.6 15.3 %fusion.113 = f32[16,512]{1,0:T(8,128)S(1)} fusion(f32[16,512,1024]{2,1,0:T(8,128)} %get-tuple-element.332, f32[16,512]{1,0:T(8,128)S(1)} %get-tuple-element.333, pred[512,1024]{1,0:T(8,128)(4,1)S(1)} %fusion.112), kind=kLoop, calls=%fused_computation.3.clone.1 | loop fusion | flops 25157632 | bytes 34144256 | tf_op jit(solution)/shard_map/while/body/eval_jaxpr/reduce_sum | solution.py:91
  228.0 14.3 %bitcast_dynamic-update-slice_fusion.6 = bf16[2,512,16,80]{1,3,2,0:T(8,128)(2,1)S(1)} fusion(bf16[2,512,16,80]{1,3,2,0:T(8,128)(2,1)S(1)} %copy-done.8, s32[]{:T(128)S(6)} %copy.79, bf16[1024,16,80]{0,2,1:T(8,128)(2,1)S(1)} %bitcast.196, f32[16,512,1024]{2,1,0:T(8,128)} %get-tuple-element.332, f32[16,512]{1,0:T(8,128)S(1)} %fusion.113, ...), kind=kOutput, calls=%fused_computation.5.clone.1 | convolution fusion | flops 1375731712 | bytes 39387140 | tf_op jit(solution)/shard_map/while/body/eval_jaxpr/hqk,khe->qhe/dot_general | solution.py:93
  250.6 9.7 multiply_reduce_fusion.3
  260.3 9.4 fusion.54
  269.7 10.1 convert_reduce_fusion.1
  279.8 4.5 multiply_reduce_fusion.1
  288.6 4.9 convolution_convert_fusion.4
  293.4 8.5 reshape.299
  302.0 7.2 copy.40
  311.0 272.4 %while.27 = (s32[]{:T(128)}, bf16[2,512,16,80]{1,3,2,0:T(8,128)(2,1)}, f32[2,1024,1280]{2,1,0:T(8,128)}, f32[2,1024,1280]{2,1,0:T(8,128)}, bf16[2,1024,1280]{1,2...) while((s32[]{:T(128)}, ...), condition=%wide.region_9.10_spmd, body=%wide.region_7.9_spmd.sunk | while | flops 6812591616 | bytes 374577376 | solution.py:170
  317.9 14.5 %fusion.123 = f32[16,512,1024]{2,1,0:T(8,128)} fusion(bf16[1024,16,80]{0,2,1:T(8,128)(2,1)S(1)} %bitcast.190, bf16[2,512,16,80]{1,3,2,0:T(8,128)(2,1)} %copy-done, s32[]{:T(128)S(6)} %copy.89), kind=kOutput, calls=%fused_computation.34.clone.1 | convolution fusion | flops 1342177280 | bytes 37486596 | tf_op jit(solution)/shard_map/while/body/eval_jaxpr/qhe,khe->hqk/dot_general | solution.py:29
  332.4 17.1 %fusion.125 = f32[16,80,1024]{2,1,0:T(8,128)} fusion(f32[16,512,1024]{2,1,0:T(8,128)} %fusion.123, f32[16,512]{1,0:T(8,128)S(1)} %dynamic-slice_bitcast_fusion.2, pred[512,1024]{1,0:T(8,128)(4,1)S(1)} %fusion.124, bf16[2,512,16,80]{1,3,2,0:T(8,128)(2,1)} %get-tuple-element.409, s32[]{:T(128)S(6)} %copy.89), kind=kOutput, calls=%fused_computation.22.clone.1 | convolution fusion | flops 1367343104 | bytes 40665092 | tf_op jit(solution)/shard_map/while/body/eval_jaxpr/hqk,qhe->khe/dot_general | solution.py:161
  349.5 5.9 copy.69
  355.4 25.5 %multiply_reduce_fusion.5 = (f32[16,512]{1,0:T(8,128)S(1)}, f32[16,512,1024]{2,1,0:T(8,128)}) fusion(f32[16,512,1024]{2,1,0:T(8,128)} %fusion.123, f32[16,512]{1,0:T(8,128)S(1)} %dynamic-slice_bitcast_fusion.2, pred[512,1024]{1,0:T(8,128)(4,1)S(1)} %fusion.124, bf16[1024,16,80]{0,2,1:T(8,128)(2,1)} %bitcast.195, ...), kind=kOutput, calls=%fused_computation.19.clone.1 | convolution fusion | flops 1375723520 | bytes 71630848 | tf_op jit(solution)/shard_map/while/body/eval_jaxpr/qhe,khe->hqk/dot_general | solution.py:150
  380.9 27.8 %multiply_convert_fusion.10 = bf16[16,512,1024]{2,1,0:T(8,128)(2,1)} fusion(f32[16,512,1024]{2,1,0:T(8,128)} %get-tuple-element.345, f32[16,512,1024]{2,1,0:T(8,128)} %fusion.123, f32[16,512]{1,0:T(8,128)S(1)} %get-tuple-element.346, f32[16,512]{1,0:T(8,128)S(1)} %dynamic-slice_bitcast_fusion.2, pred[512,1024]{1,0:T(8,128)(4,1)S(1)} %fusion.124), kind=kLoop, calls=%fused_computation.18.clone.1 | loop fusion | flops 41943040 | bytes 84475904 | tf_op jit(solution)/shard_map/while/body/eval_jaxpr/convert_element_type | solution.py:154
  408.7 12.1 %bitcast_dynamic-update-slice_fusion.8 = bf16[2,512,16,80]{1,3,2,0:T(8,128)(2,1)} fusion(bf16[2,512,16,80]{1,3,2,0:T(8,128)(2,1)} %get-tuple-element.389, s32[]{:T(128)S(6)} %copy.89, bf16[1024,16,80]{0,2,1:T(8,128)(2,1)S(1)} %bitcast.191, bf16[16,512,1024]{2,1,0:T(8,128)(2,1)} %multiply_convert_fusion.10), kind=kOutput, calls=%fused_computation.26.clone.1 | convolution fusion | flops 1342177280 | bytes 22020100 | tf_op jit(solution)/shard_map/while/body/eval_jaxpr/hqk,khe->qhe/dot_general | solution.py:155
  420.8 11.6 %fusion.126 = f32[16,80,1024]{2,1,0:T(8,128)} fusion(bf16[16,512,1024]{2,1,0:T(8,128)(2,1)} %multiply_convert_fusion.10, bf16[2,512,16,80]{1,3,2,0:T(8,128)(2,1)} %copy-done, s32[]{:T(128)S(6)} %copy.89), kind=kOutput, calls=%fused_computation.32.clone.1 | convolution fusion | flops 1342177280 | bytes 23330820 | tf_op jit(solution)/shard_map/while/body/eval_jaxpr/hqk,qhe->khe/dot_general | solution.py:158
  432.4 5.9 copy.70
  438.4 8.8 constant_dynamic-update-slice_fusion.3
  453.8 14.5 %fusion.123 = f32[16,512,1024]{2,1,0:T(8,128)} fusion(bf16[1024,16,80]{0,2,1:T(8,128)(2,1)S(1)} %bitcast.190, bf16[2,512,16,80]{1,3,2,0:T(8,128)(2,1)} %copy-done, s32[]{:T(128)S(6)} %copy.89), kind=kOutput, calls=%fused_computation.34.clone.1 | convolution fusion | flops 1342177280 | bytes 37486596 | tf_op jit(solution)/shard_map/while/body/eval_jaxpr/qhe,khe->hqk/dot_general | solution.py:29
  468.4 17.1 %fusion.125 = f32[16,80,1024]{2,1,0:T(8,128)} fusion(f32[16,512,1024]{2,1,0:T(8,128)} %fusion.123, f32[16,512]{1,0:T(8,128)S(1)} %dynamic-slice_bitcast_fusion.2, pred[512,1024]{1,0:T(8,128)(4,1)S(1)} %fusion.124, bf16[2,512,16,80]{1,3,2,0:T(8,128)(2,1)} %get-tuple-element.409, s32[]{:T(128)S(6)} %copy.89), kind=kOutput, calls=%fused_computation.22.clone.1 | convolution fusion | flops 1367343104 | bytes 40665092 | tf_op jit(solution)/shard_map/while/body/eval_jaxpr/hqk,qhe->khe/dot_general | solution.py:161
  485.5 5.9 copy.69
  491.3 25.5 %multiply_reduce_fusion.5 = (f32[16,512]{1,0:T(8,128)S(1)}, f32[16,512,1024]{2,1,0:T(8,128)}) fusion(f32[16,512,1024]{2,1,0:T(8,128)} %fusion.123, f32[16,512]{1,0:T(8,128)S(1)} %dynamic-slice_bitcast_fusion.2, pred[512,1024]{1,0:T(8,128)(4,1)S(1)} %fusion.124, bf16[1024,16,80]{0,2,1:T(8,128)(2,1)} %bitcast.195, ...), kind=kOutput, calls=%fused_computation.19.clone.1 | convolution fusion | flops 1375723520 | bytes 71630848 | tf_op jit(solution)/shard_map/while/body/eval_jaxpr/qhe,khe->hqk/dot_general | solution.py:150
  516.8 27.8 %multiply_convert_fusion.10 = bf16[16,512,1024]{2,1,0:T(8,128)(2,1)} fusion(f32[16,512,1024]{2,1,0:T(8,128)} %get-tuple-element.345, f32[16,512,1024]{2,1,0:T(8,128)} %fusion.123, f32[16,512]{1,0:T(8,128)S(1)} %get-tuple-element.346, f32[16,512]{1,0:T(8,128)S(1)} %dynamic-slice_bitcast_fusion.2, pred[512,1024]{1,0:T(8,128)(4,1)S(1)} %fusion.124), kind=kLoop, calls=%fused_computation.18.clone.1 | loop fusion | flops 41943040 | bytes 84475904 | tf_op jit(solution)/shard_map/while/body/eval_jaxpr/convert_element_type | solution.py:154
  544.7 12.0 %bitcast_dynamic-update-slice_fusion.8 = bf16[2,512,16,80]{1,3,2,0:T(8,128)(2,1)} fusion(bf16[2,512,16,80]{1,3,2,0:T(8,128)(2,1)} %get-tuple-element.389, s32[]{:T(128)S(6)} %copy.89, bf16[1024,16,80]{0,2,1:T(8,128)(2,1)S(1)} %bitcast.191, bf16[16,512,1024]{2,1,0:T(8,128)(2,1)} %multiply_convert_fusion.10), kind=kOutput, calls=%fused_computation.26.clone.1 | convolution fusion | flops 1342177280 | bytes 22020100 | tf_op jit(solution)/shard_map/while/body/eval_jaxpr/hqk,khe->qhe/dot_general | solution.py:155
  556.7 11.6 %fusion.126 = f32[16,80,1024]{2,1,0:T(8,128)} fusion(bf16[16,512,1024]{2,1,0:T(8,128)(2,1)} %multiply_convert_fusion.10, bf16[2,512,16,80]{1,3,2,0:T(8,128)(2,1)} %copy-done, s32[]{:T(128)S(6)} %copy.89), kind=kOutput, calls=%fused_computation.32.clone.1 | convolution fusion | flops 1342177280 | bytes 23330820 | tf_op jit(solution)/shard_map/while/body/eval_jaxpr/hqk,qhe->khe/dot_general | solution.py:158
  568.3 5.9 copy.70
  574.2 8.7 constant_dynamic-update-slice_fusion.3
  585.2 9.0 convolution_convert_fusion
  594.3 11.4 %convolution_convert_fusion.1 = bf16[1280,1280]{1,0:T(8,128)(2,1)} fusion(bf16[1024,1280]{1,0:T(8,128)(2,1)} %copy-done.47, f32[1024,1280]{1,0:T(8,128)} %get-tuple-element.212, f32[1280]{0:T(1024)S(1)} %copy-done.32, f32[1024]{0:T(1024)S(1)} %copy-done.30), kind=kOutput, calls=%fused_computation.57 | convolution fusion | flops 3361013760 | bytes 11150336 | tf_op jit(solution)/shard_map/nd,nf->df/dot_general | solution.py:130
  605.8 7.4 convolution_convert_fusion.2
  613.5 6.3 fusion.34
  624.9 5.1 convolution_convert_fusion.3
  634.3 5.1 fusion.32
  643.7 7.7 fusion.31
  652.2 8.7 fusion.55
  660.9 6.0 reduce-scatter.23.cloned.1.call-done
  667.0 41.2 %reduce-scatter.21.cloned.1.call-done = bf16[320,1280]{1,0:T(8,128)(2,1)} async-done(((bf16[1280,1280]{1,0:T(8,128)(2,1)}), bf16[320,1280]{1,0:T(8,128)(2,1)}) %reduce-scatter.21.cloned.1.call-update) | async-done | bytes 819216 | tf_op jit(solution)/shard_map/reduce_scatter | solution.py:213
  708.1 41.3 %reduce-scatter.19.cloned.1.call-done = bf16[320,1280]{1,0:T(8,128)(2,1)} async-done(((bf16[1280,1280]{1,0:T(8,128)(2,1)}), bf16[320,1280]{1,0:T(8,128)(2,1)}) %reduce-scatter.19.cloned.1.call-update) | async-done | bytes 819216 | tf_op jit(solution)/shard_map/reduce_scatter | solution.py:210
  749.4 41.2 %reduce-scatter.13.cloned.1.call-done = bf16[320,1280]{1,0:T(8,128)(2,1)} async-done(((bf16[1280,1280]{1,0:T(8,128)(2,1)}), bf16[320,1280]{1,0:T(8,128)(2,1)}) %reduce-scatter.13.cloned.1.call-update) | async-done | bytes 819216 | tf_op jit(solution)/shard_map/reduce_scatter | solution.py:201
  790.6 41.1 %reduce-scatter.17.cloned.1.call-done = bf16[320,1280]{1,0:T(8,128)(2,1)} async-done(((bf16[1280,1280]{1,0:T(8,128)(2,1)}), bf16[320,1280]{1,0:T(8,128)(2,1)}) %reduce-scatter.17.cloned.1.call-update) | async-done | bytes 819216 | tf_op jit(solution)/shard_map/reduce_scatter | solution.py:207
  831.7 41.2 %reduce-scatter.15.cloned.1.call-done = bf16[320,1280]{1,0:T(8,128)(2,1)} async-done(((bf16[1280,1280]{1,0:T(8,128)(2,1)}), bf16[320,1280]{1,0:T(8,128)(2,1)}) %reduce-scatter.15.cloned.1.call-update) | async-done | bytes 819216 | tf_op jit(solution)/shard_map/reduce_scatter | solution.py:204
  872.9 10.9 %add_convert_fusion = bf16[1024,1280]{1,0:T(8,128)(2,1)} fusion(f32[1024,1280]{1,0:T(8,128)} %get-tuple-element.212, bf16[1280,1280]{1,0:T(8,128)(2,1)} %all-gather.23.cloned.1.call-done, f32[1280]{0:T(1024)S(1)} %copy-done.40, f32[1024,1280]{1,0:T(8,128)} %fusion.54, f32[1280]{0:T(1024)S(1)} %copy-done.42), kind=kOutput, calls=%fused_computation.90 | convolution fusion | flops 3367239680 | bytes 16394240 | tf_op jit(solution)/shard_map/dot_general | solution.py:108
  888.9 6.3 fusion.46
  895.2 46.5 %all-reduce = (f32[1280]{0:T(1024)}, f32[1280]{0:T(1024)}, f32[1280]{0:T(1024)}, f32[1280]{0:T(1024)}, f32[80]{0:T(128)}) all-reduce(f32[1280]{0:T(1024)S(1)} %copy-done.33, f32[1280]{0:T(1024)S(1)} %convert_reduce_fusion, f32[1280]{0:T(1024)S(1)} %get-tuple-element.144, ...), channel_id=1, replica_groups=mesh['rep'=8,'fsdp'=2,'ctx'=2] {'rep','fsdp','ctx'}, use_global_device_ids=true, to_apply=%region_24.25 | all-reduce | flops 5200 | bytes 41600 | tf_op jit(solution)/shard_map/psum | solution.py:228
  941.7 6.0 fusion.43
  947.7 105.4 %all-reduce.4.cloned.1.call-done = (bf16[320,1280]{1,0:T(8,128)(2,1)}, bf16[320,1280]{1,0:T(8,128)(2,1)}, bf16[320,1280]{1,0:T(8,128)(2,1)}, bf16[320,1280]{1,0:...) async-done(((bf16[320,1280]{1,0:T(8,128)(2,1)}, bf16[320,1280]{1,0:T(8,128)(2,1)}, bf16[320,1280]{1,0:T(8,128)(2,1)}, bf16[320,1280]{1,0:T(8,128)(2,1)}, ...) | async-done | bytes 4915216 | tf_op jit(solution)/shard_map/psum | solution.py:221
  (203 shorter events, 80.0 us)
Async XLA Ops:
  7.2 5.2 copy-start.3
  7.2 34.4 %all-gather.15.cloned.1.call-start = ((), (), s32[]{:S(2)}) async-start(), calls=%async_computation.11 | async-start | bytes 4096000 | tf_op jit(solution)/shard_map/all_gather | solution.py:55
  7.9 64.5 %all-gather.9.cloned.1.call-start = ((), (), s32[]{:S(2)}) async-start(), calls=%async_computation.8 | async-start | bytes 4096000 | tf_op jit(solution)/shard_map/all_gather | solution.py:56
  8.7 94.6 %all-gather.13.cloned.1.call-start = ((), (), s32[]{:S(2)}) async-start(), calls=%async_computation.10 | async-start | bytes 4096000 | tf_op jit(solution)/shard_map/all_gather | solution.py:54
  9.4 110.5 %all-gather.17.cloned.1.call-start = ((), (), s32[]{:S(2)}) async-start(), calls=%async_computation.12 | async-start | bytes 7864320 | tf_op jit(solution)/shard_map/all_gather | solution.py:80
  53.9 84.4 %all-gather.11.cloned.1.call-start = ((), (), s32[]{:S(2)}) async-start(), calls=%async_computation.9 | async-start | bytes 7864320 | tf_op jit(solution)/shard_map/all_gather | solution.py:81
  80.2 6.9 copy-start.44
  80.2 6.9 copy-start.25
  84.7 165.9 %all-gather.19.cloned.1.call-start = ((), (), s32[]{:S(2)}) async-start(), calls=%async_computation.13 | async-start | bytes 4096000 | tf_op jit(solution)/shard_map/all_gather | solution.py:57
  85.3 175.0 %all-gather.21.cloned.1.call-start = ((), (), s32[]{:S(2)}) async-start(), calls=%async_computation.14 | async-start | bytes 4096000 | tf_op jit(solution)/shard_map/all_gather | solution.py:58
  86.1 183.7 %all-gather.23.cloned.1.call-start = ((), (), s32[]{:S(2)}) async-start(), calls=%async_computation.15 | async-start | bytes 4096000 | tf_op jit(solution)/shard_map/all_gather | solution.py:59
  86.8 543.3 %reduce-scatter.11.cloned.1.call-start = ((), (), s32[]{:S(2)}) async-start(), calls=%async_computation.17 | async-start | bytes 15728640 | tf_op jit(solution)/shard_map/reduce_scatter | solution.py:175
  87.1 21.8 %copy-start.35 = (f32[80]{0:T(128)}, f32[80]{0:T(128)S(1)}, u32[]{:S(2)}) copy-start(f32[80]{0:T(128)S(1)} %fusion.51) | copy-start | bytes 964
  108.9 31.2 %copy-start.43 = (s32[2]{0:T(128)S(1)}, s32[2]{0:T(128)}, u32[]{:S(2)}) copy-start(s32[2]{0:T(128)} %param.19) | copy-start | bytes 28
  159.9 15.4 %copy-start.5 = (bf16[1,1024,1280]{1,2,0:T(8,128)(2,1)S(1)}, bf16[1,1024,1280]{1,2,0:T(8,128)(2,1)}, u32[]{:S(2)}) copy-start(bf16[1,1024,1280]{1,2,0:T(8,128)(2,1)} %get-tuple-element.330) | copy-start | bytes 7864324 | tf_op jit(solution)/shard_map/while
  159.9 15.4 %copy-start.8 = (bf16[2,512,16,80]{1,3,2,0:T(8,128)(2,1)S(1)}, bf16[2,512,16,80]{1,3,2,0:T(8,128)(2,1)}, u32[]{:S(2)}) copy-start(bf16[2,512,16,80]{1,3,2,0:T(8,128)(2,1)} %get-tuple-element.359) | copy-start | bytes 7864324 | tf_op jit(solution)/shard_map/while
  212.6 15.4 %copy-start.5 = (bf16[1,1024,1280]{1,2,0:T(8,128)(2,1)S(1)}, bf16[1,1024,1280]{1,2,0:T(8,128)(2,1)}, u32[]{:S(2)}) copy-start(bf16[1,1024,1280]{1,2,0:T(8,128)(2,1)} %get-tuple-element.330) | copy-start | bytes 7864324 | tf_op jit(solution)/shard_map/while
  212.6 15.4 %copy-start.8 = (bf16[2,512,16,80]{1,3,2,0:T(8,128)(2,1)S(1)}, bf16[2,512,16,80]{1,3,2,0:T(8,128)(2,1)}, u32[]{:S(2)}) copy-start(bf16[2,512,16,80]{1,3,2,0:T(8,128)(2,1)} %get-tuple-element.359) | copy-start | bytes 7864324 | tf_op jit(solution)/shard_map/while
  250.6 9.7 copy-start.31
  260.3 24.0 %copy-start.29 = (f32[1024]{0:T(1024)}, f32[1024]{0:T(1024)S(1)}, u32[]{:S(2)}) copy-start(f32[1024]{0:T(1024)S(1)} %get-tuple-element.206) | copy-start | bytes 12292
  260.3 9.4 copy-start.41
  269.7 10.1 copy-start.7
  269.7 10.1 copy-start.39
  279.8 4.5 copy-start.47
  279.8 4.5 copy-start.11
  284.3 4.3 copy-start.14
  286.2 2.4 copy-start.6
  311.2 6.5 copy-start
  311.2 6.4 copy-start.2
  438.3 8.8 copy-start.1
  447.2 6.4 copy-start
  447.2 6.4 copy-start.2
  574.2 8.8 copy-start.1
  583.4 56.1 %reduce-scatter.9.cloned.1.call-start = ((), (), s32[]{:S(2)}) async-start(), calls=%async_computation.16 | async-start | bytes 15728640 | tf_op jit(solution)/shard_map/reduce_scatter | solution.py:174
  583.5 1.7 copy-start.12
  583.5 1.7 copy-start.42
  584.0 10.3 copy-start.30
  584.0 10.3 copy-start.32
  584.0 82.9 %reduce-scatter.23.cloned.1.call-start = ((), (), s32[]{:S(2)}) async-start(), calls=%async_computation.23 | async-start | bytes 4096000 | tf_op jit(solution)/shard_map/reduce_scatter | solution.py:216
  594.2 11.6 %copy-start.10 = (bf16[160,8,2,512]{3,1,2,0:T(8,128)(2,1)S(1)}, bf16[160,8,2,512]{3,1,2,0:T(8,128)(2,1)}, u32[]{:S(2)}) copy-start(bf16[160,8,2,512]{3,1,2,0:T(8,128)(2,1)} %copy.65) | copy-start | bytes 7864324
  594.3 113.9 %reduce-scatter.21.cloned.1.call-start = ((), (), s32[]{:S(2)}) async-start(), calls=%async_computation.22 | async-start | bytes 4096000 | tf_op jit(solution)/shard_map/reduce_scatter | solution.py:213
  605.8 7.8 copy-start.36
  605.8 143.6 %reduce-scatter.19.cloned.1.call-start = ((), (), s32[]{:S(2)}) async-start(), calls=%async_computation.21 | async-start | bytes 4096000 | tf_op jit(solution)/shard_map/reduce_scatter | solution.py:210
  613.3 177.3 %reduce-scatter.13.cloned.1.call-start = ((), (), s32[]{:S(2)}) async-start(), calls=%async_computation.18 | async-start | bytes 4096000 | tf_op jit(solution)/shard_map/reduce_scatter | solution.py:201
  619.9 5.0 copy-start.16
  630.0 201.7 %reduce-scatter.17.cloned.1.call-start = ((), (), s32[]{:S(2)}) async-start(), calls=%async_computation.20 | async-start | bytes 4096000 | tf_op jit(solution)/shard_map/reduce_scatter | solution.py:207
  639.4 233.5 %reduce-scatter.15.cloned.1.call-start = ((), (), s32[]{:S(2)}) async-start(), calls=%async_computation.19 | async-start | bytes 4096000 | tf_op jit(solution)/shard_map/reduce_scatter | solution.py:204
  643.7 8.0 copy-start.28
  643.7 8.0 copy-start.13
  651.4 401.7 %all-reduce.4.cloned.1.call-start = ((), (), s32[]{:S(2)}) async-start(), calls=%async_computation.24 | async-start | bytes 9830400 | tf_op jit(solution)/shard_map/psum | solution.py:221
  652.2 220.7 %copy-start.40 = (f32[1280]{0:T(1024)S(1)}, f32[1280]{0:T(1024)}, u32[]{:S(2)}) copy-start(f32[1280]{0:T(1024)} %param.27) | copy-start | bytes 15364
  872.9 10.9 %copy-start.20 = (bf16[2,512,1280]{2,1,0:T(8,128)(2,1)S(1)}, bf16[2,512,1280]{2,1,0:T(8,128)(2,1)}, u32[]{:S(2)}) copy-start(bf16[2,512,1280]{2,1,0:T(8,128)(2,1)} %copy-done.19) | copy-start | bytes 7864324
  872.9 10.9 %copy-start.37 = (bf16[1280,1280]{1,0:T(8,128)(2,1)S(1)}, bf16[1280,1280]{1,0:T(8,128)(2,1)}, u32[]{:S(2)}) copy-start(bf16[1280,1280]{1,0:T(8,128)(2,1)} %all-gather.15.cloned.1.call-done) | copy-start | bytes 9830404
  883.8 3.6 copy-start.4
  883.8 3.6 copy-start.18
  883.8 3.6 copy-start.26
  883.9 3.6 copy-start.38
  883.9 5.0 copy-start.46
  888.9 6.3 copy-start.33
  888.9 6.3 copy-start.34
  1053.1 5.1 copy-start.24
  1053.1 6.3 copy-start.23
  1053.1 7.6 copy-start.22
  1055.7 6.3 copy-start.21
  (7 other events, 8.9 us)
Sparse Core Ops, SparseCore 0:
  9.6 31.9 all-gather.14
  43.1 29.2 all-gather.8
  74.0 29.2 all-gather.12
  104.7 15.2 all-gather.16
  121.9 16.3 all-gather.10
  139.7 30.4 all-gather.18
  171.7 29.2 all-gather.20
  202.6 29.2 all-gather.22
  583.5 19.3 reduce-scatter.10
  605.0 19.2 reduce-scatter.8
  626.9 39.9 reduce-scatter.22
  669.4 38.6 reduce-scatter.20
  710.7 38.6 reduce-scatter.18
  751.8 38.6 reduce-scatter.12
  793.0 38.6 reduce-scatter.16
  834.1 38.6 reduce-scatter.14
  877.1 175.9 all-reduce.3
where the time goes:
time: 1080 us; the launch traced here: 1070 us
  waiting for transfers between devices  401 us (37%)
  matrix products  357 us (33%)
  other arithmetic  131 us (12%)
  local copies, waits for them, and re-layouts  118 us (11%)
  blocking collectives  46.5 us (4%)
  between operations  14.7 us (1%)
    psum x1, waiting for transfers between devices, shards(): lax.psum(query_shard.astype(jnp.bfloat16), 'rep').astype(jnp.float32)  105 us
    dot_general x4, matrix products, masked_scores(): jnp.einsum('qhe,khe->hqk', queries, keys, preferred_element_type=jnp.floa...  57 us
    convert_element_type x2, other arithmetic, backward_one(): score_grad = (exact_prob * (prob_grad - row_inner)).astype(jnp.bfloat16)  55.7 us
    dot_general x2, matrix products, backward_one(): jnp.einsum('qhe,khe->hqk', grad_seq, values_heads, preferred_element_type...  51 us
    psum x1, blocking collectives, shards(): lax.psum((upbias_part, downbias_part, attngain_part, mlpgain_part, scale_...  46.5 us
    reduce_scatter x1, waiting for transfers between devices, shards(): lax.psum_scatter(output_part.astype(jnp.bfloat16), ('fsdp', 'ctx'), scatt...  41.3 us
    dynamic_update_slice x6, local copies, waits for them, and re-layouts, shards(): lax.map(backward_one, (queries, key_back, value_back, context_grad, logsu...  41.2 us
    reduce_scatter x1, waiting for transfers between devices, shards(): lax.psum_scatter(up_part.astype(jnp.bfloat16), ('fsdp', 'ctx'), scatter_d...  41.2 us
  transfers between devices with their start and end apart: 17, of which 12 were waited for; matrix products, arithmetic and copies ran while one was open for 25% of the time, Pallas kernels for 0%

commit v1 on v0

--- a/solution.py
+++ b/solution.py
@@ -50,9 +50,30 @@
     head_count = model_width // HD
     position_index = lax.axis_index("ctx")
     offset = position_index * local_rows
+
+    def _set_region(page):
+        b_next = lax.axis_size(("fsdp", "ctx"))
+        tmp, block_out, part_next = (b_next, lax.axis_index(("fsdp", "ctx")), page.shape[0])
+        top, found_now = (page, 1)
+        while found_now < tmp:
+            top = jnp.concatenate(
+                [
+                    top,
+                    lax.ppermute(
+                        top,
+                        axis_name=("fsdp", "ctx"),
+                        perm=[(j0, (j0 - found_now) % tmp) for j0 in range(tmp)],
+                    ),
+                ],
+                axis=0,
+            )
+            found_now = 2 * found_now
+        long_array = jnp.roll(top, shift=block_out * part_next, axis=0)
+        return long_array
+
     full_query, full_key, full_value, full_output, full_up, full_down = (
         lax.all_gather(query_weight, ("fsdp", "ctx"), axis=0, tiled=True),
-        lax.all_gather(key_weight, ("fsdp", "ctx"), axis=0, tiled=True),
+        _set_region(key_weight),
         lax.all_gather(value_weight, ("fsdp", "ctx"), axis=0, tiled=True),
         lax.all_gather(output_weight, ("fsdp", "ctx"), axis=0, tiled=True),
         lax.all_gather(up_weight, ("fsdp", "ctx"), axis=0, tiled=True),

time: 1080 us -> 1100 us (1.019)
  waiting for transfers between devices: 401 us -> 425 us
    ppermute x0 -> x2, waiting for transfers between devices: none -> 67.9 us  [_set_region(): lax.ppermute(top, axis_name=('fsdp', 'ctx'), perm=[(j0, (j0 - found_now)...]
    all_gather x1, waiting for transfers between devices: 18.5 us -> 0.02 us  [shards(): lax.all_gather(value_weight, ('fsdp', 'ctx'), axis=0, tiled=True)]
    all_gather x1, waiting for transfers between devices: 14 us -> 0.01 us  [shards(): lax.all_gather(query_weight, ('fsdp', 'ctx'), axis=0, tiled=True)]
    all_gather x1, waiting for transfers between devices: 18.4 us -> 4.71 us  [shards(): lax.all_gather(value_local, 'ctx', axis=1, tiled=True)]
  transfers between devices with their start and end apart: 17 -> 19, of which waited for: 12 -> 11; matrix products, arithmetic and copies ran while one was open for 25% -> 25% of each run, Pallas kernels for 0% -> 0%
where the time goes in v1:
time: 1100 us
  waiting for transfers between devices  425 us (39%)
  matrix products  354 us (32%)
  other arithmetic  129 us (12%)
  local copies, waits for them, and re-layouts  123 us (11%)
  blocking collectives  46.6 us (4%)
  between operations  14.8 us (1%)
    psum x1, waiting for transfers between devices, shards(): lax.psum(query_shard.astype(jnp.bfloat16), 'rep').astype(jnp.float32)  115 us
    ppermute x2, waiting for transfers between devices, _set_region(): lax.ppermute(top, axis_name=('fsdp', 'ctx'), perm=[(j0, (j0 - found_now)...  67.9 us
    dot_general x4, matrix products, masked_scores(): jnp.einsum('qhe,khe->hqk', queries, keys, preferred_element_type=jnp.floa...  56.9 us
    convert_element_type x2, other arithmetic, backward_one(): score_grad = (exact_prob * (prob_grad - row_inner)).astype(jnp.bfloat16)  55.7 us
    dot_general x2, matrix products, backward_one(): jnp.einsum('qhe,khe->hqk', grad_seq, values_heads, preferred_element_type...  50.8 us
    psum x1, blocking collectives, shards(): lax.psum((upbias_part, downbias_part, attngain_part, mlpgain_part, scale_...  46.6 us
    reduce_scatter x1, waiting for transfers between devices, shards(): lax.psum_scatter(up_part.astype(jnp.bfloat16), ('fsdp', 'ctx'), scatter_d...  41.3 us
    reduce_scatter x1, waiting for transfers between devices, shards(): lax.psum_scatter(query_part.astype(jnp.bfloat16), ('fsdp', 'ctx'), scatte...  41.3 us
  transfers between devices with their start and end apart: 19, of which 11 were waited for; matrix products, arithmetic and copies ran while one was open for 25% of the time, Pallas kernels for 0%

profile of v1, /device:TPU:0, one launch (start us, length us, event | category | flops | bytes accessed | tf_op | source)
XLA Modules:
  0.0 1097.3 jit_solution(15169955081369782000)
XLA Ops:
  11.2 12.0 %collective-permute-done = bf16[320,1280]{1,0:T(8,128)(2,1)} collective-permute-done((bf16[320,1280]{1,0:T(8,128)(2,1)}, bf16[320,1280]{1,0:T(8,128)(2,1)}, u32[]{:S(2)}, u32[]{:S(2)}) %collective-permute-start) | collective-permute-done | bytes 819232 | tf_op jit(solution)/shard_map/ppermute | solution.py:62
  29.1 55.9 %collective-permute-done.1 = bf16[640,1280]{1,0:T(8,128)(2,1)} collective-permute-done((bf16[640,1280]{1,0:T(8,128)(2,1)}, bf16[640,1280]{1,0:T(8,128)(2,1)}, u32[]{:S(2)}, u32[]{:S(2)}) %collective-permute-start.1) | collective-permute-done | bytes 1638432 | tf_op jit(solution)/shard_map/ppermute | solution.py:62
  89.3 4.9 convolution_convert_fusion.5
  98.8 7.8 convolution_convert_fusion.6
  106.6 4.6 copy.35
  115.5 5.6 copy.36
  121.2 9.0 multiply_convert_fusion.4
  130.1 4.7 all-gather.11.cloned.1.call-done
  136.6 103.9 %while.26 = (s32[]{:T(128)}, bf16[2,512,16,80]{1,3,2,0:T(8,128)(2,1)}, f32[2,16,512,1]{2,1,3,0:T(8,128)S(1)}, bf16[2,1024,1280]{1,2,0:T(8,128)(2,1)}, s32[]{:T(1...) while((s32[]{:T(128)}, ...), condition=%wide.region_4.5_spmd, body=%wide.region_1.4_spmd.sunk | while | flops 2760893952 | bytes 154147024 | solution.py:122
  138.3 4.6 constant_dynamic-slice_fusion.7
  142.9 13.5 %select_reduce_fusion.2 = (f32[16,512]{1,0:T(8,128)S(1)}, f32[16,512,1024]{2,1,0:T(8,128)}) fusion(pred[512,1024]{1,0:T(8,128)(4,1)S(1)} %fusion.113, bf16[1024,16,80]{0,2,1:T(8,128)(2,1)S(1)} %bitcast.192, bf16[2,512,16,80]{1,3,2,0:T(8,128)(2,1)S(1)} %get-tuple-element.373, s32[]{:T(128)S(6)} %copy.84), kind=kOutput, calls=%fused_computation.2.clone.1 | convolution fusion | flops 1358946304 | bytes 38043652 | tf_op jit(solution)/shard_map/while/body/eval_jaxpr/qhe,khe->hqk/dot_general | solution.py:29
  156.4 15.4 %fusion.114 = f32[16,512]{1,0:T(8,128)S(1)} fusion(f32[16,512,1024]{2,1,0:T(8,128)} %get-tuple-element.332, f32[16,512]{1,0:T(8,128)S(1)} %get-tuple-element.333, pred[512,1024]{1,0:T(8,128)(4,1)S(1)} %fusion.113), kind=kLoop, calls=%fused_computation.3.clone.1 | loop fusion | flops 25157632 | bytes 34144256 | tf_op jit(solution)/shard_map/while/body/eval_jaxpr/reduce_sum | solution.py:112
  171.8 15.2 %bitcast_dynamic-update-slice_fusion.6 = bf16[2,512,16,80]{1,3,2,0:T(8,128)(2,1)S(1)} fusion(bf16[2,512,16,80]{1,3,2,0:T(8,128)(2,1)S(1)} %copy-done.9, s32[]{:T(128)S(6)} %copy.84, bf16[1024,16,80]{0,2,1:T(8,128)(2,1)S(1)} %bitcast.195, f32[16,512,1024]{2,1,0:T(8,128)} %get-tuple-element.332, f32[16,512]{1,0:T(8,128)S(1)} %fusion.114, ...), kind=kOutput, calls=%fused_computation.5.clone.1 | convolution fusion | flops 1375731712 | bytes 39387140 | tf_op jit(solution)/shard_map/while/body/eval_jaxpr/hqk,khe->qhe/dot_general | solution.py:114
  190.2 4.6 constant_dynamic-slice_fusion.7
  194.8 14.3 %select_reduce_fusion.2 = (f32[16,512]{1,0:T(8,128)S(1)}, f32[16,512,1024]{2,1,0:T(8,128)}) fusion(pred[512,1024]{1,0:T(8,128)(4,1)S(1)} %fusion.113, bf16[1024,16,80]{0,2,1:T(8,128)(2,1)S(1)} %bitcast.192, bf16[2,512,16,80]{1,3,2,0:T(8,128)(2,1)S(1)} %get-tuple-element.373, s32[]{:T(128)S(6)} %copy.84), kind=kOutput, calls=%fused_computation.2.clone.1 | convolution fusion | flops 1358946304 | bytes 38043652 | tf_op jit(solution)/shard_map/while/body/eval_jaxpr/qhe,khe->hqk/dot_general | solution.py:29
  209.2 15.3 %fusion.114 = f32[16,512]{1,0:T(8,128)S(1)} fusion(f32[16,512,1024]{2,1,0:T(8,128)} %get-tuple-element.332, f32[16,512]{1,0:T(8,128)S(1)} %get-tuple-element.333, pred[512,1024]{1,0:T(8,128)(4,1)S(1)} %fusion.113), kind=kLoop, calls=%fused_computation.3.clone.1 | loop fusion | flops 25157632 | bytes 34144256 | tf_op jit(solution)/shard_map/while/body/eval_jaxpr/reduce_sum | solution.py:112
  224.6 14.3 %bitcast_dynamic-update-slice_fusion.6 = bf16[2,512,16,80]{1,3,2,0:T(8,128)(2,1)S(1)} fusion(bf16[2,512,16,80]{1,3,2,0:T(8,128)(2,1)S(1)} %copy-done.9, s32[]{:T(128)S(6)} %copy.84, bf16[1024,16,80]{0,2,1:T(8,128)(2,1)S(1)} %bitcast.195, f32[16,512,1024]{2,1,0:T(8,128)} %get-tuple-element.332, f32[16,512]{1,0:T(8,128)S(1)} %fusion.114, ...), kind=kOutput, calls=%fused_computation.5.clone.1 | convolution fusion | flops 1375731712 | bytes 39387140 | tf_op jit(solution)/shard_map/while/body/eval_jaxpr/hqk,khe->qhe/dot_general | solution.py:114
  247.2 9.7 multiply_reduce_fusion.3
  256.9 9.4 fusion.56
  266.3 10.0 convert_reduce_fusion.1
  276.4 4.5 multiply_reduce_fusion.1
  285.1 4.9 convolution_convert_fusion.4
  290.0 8.5 reshape.299
  298.5 7.2 copy.40
  307.5 272.2 %while.27 = (s32[]{:T(128)}, bf16[2,512,16,80]{1,3,2,0:T(8,128)(2,1)}, f32[2,1024,1280]{2,1,0:T(8,128)}, f32[2,1024,1280]{2,1,0:T(8,128)}, bf16[2,1024,1280]{1,2...) while((s32[]{:T(128)}, ...), condition=%wide.region_9.10_spmd, body=%wide.region_7.9_spmd.sunk | while | flops 6812591616 | bytes 374577376 | solution.py:191
  314.4 14.5 %fusion.124 = f32[16,512,1024]{2,1,0:T(8,128)} fusion(bf16[1024,16,80]{0,2,1:T(8,128)(2,1)S(1)} %bitcast.189, bf16[2,512,16,80]{1,3,2,0:T(8,128)(2,1)} %copy-done, s32[]{:T(128)S(6)} %copy.94), kind=kOutput, calls=%fused_computation.34.clone.1 | convolution fusion | flops 1342177280 | bytes 37486596 | tf_op jit(solution)/shard_map/while/body/eval_jaxpr/qhe,khe->hqk/dot_general | solution.py:29
  328.9 17.1 %fusion.126 = f32[16,80,1024]{2,1,0:T(8,128)} fusion(f32[16,512,1024]{2,1,0:T(8,128)} %fusion.124, f32[16,512]{1,0:T(8,128)S(1)} %dynamic-slice_bitcast_fusion.2, pred[512,1024]{1,0:T(8,128)(4,1)S(1)} %fusion.125, bf16[2,512,16,80]{1,3,2,0:T(8,128)(2,1)} %get-tuple-element.409, s32[]{:T(128)S(6)} %copy.94), kind=kOutput, calls=%fused_computation.22.clone.1 | convolution fusion | flops 1367343104 | bytes 40665092 | tf_op jit(solution)/shard_map/while/body/eval_jaxpr/hqk,qhe->khe/dot_general | solution.py:182
  346.0 5.9 copy.69
  351.9 25.4 %multiply_reduce_fusion.5 = (f32[16,512]{1,0:T(8,128)S(1)}, f32[16,512,1024]{2,1,0:T(8,128)}) fusion(f32[16,512,1024]{2,1,0:T(8,128)} %fusion.124, f32[16,512]{1,0:T(8,128)S(1)} %dynamic-slice_bitcast_fusion.2, pred[512,1024]{1,0:T(8,128)(4,1)S(1)} %fusion.125, bf16[1024,16,80]{0,2,1:T(8,128)(2,1)} %bitcast.194, ...), kind=kOutput, calls=%fused_computation.19.clone.1 | convolution fusion | flops 1375723520 | bytes 71630848 | tf_op jit(solution)/shard_map/while/body/eval_jaxpr/qhe,khe->hqk/dot_general | solution.py:171
  377.3 27.9 %multiply_convert_fusion.10 = bf16[16,512,1024]{2,1,0:T(8,128)(2,1)} fusion(f32[16,512,1024]{2,1,0:T(8,128)} %get-tuple-element.345, f32[16,512,1024]{2,1,0:T(8,128)} %fusion.124, f32[16,512]{1,0:T(8,128)S(1)} %get-tuple-element.346, f32[16,512]{1,0:T(8,128)S(1)} %dynamic-slice_bitcast_fusion.2, pred[512,1024]{1,0:T(8,128)(4,1)S(1)} %fusion.125), kind=kLoop, calls=%fused_computation.18.clone.1 | loop fusion | flops 41943040 | bytes 84475904 | tf_op jit(solution)/shard_map/while/body/eval_jaxpr/convert_element_type | solution.py:175
  405.1 12.0 %bitcast_dynamic-update-slice_fusion.8 = bf16[2,512,16,80]{1,3,2,0:T(8,128)(2,1)} fusion(bf16[2,512,16,80]{1,3,2,0:T(8,128)(2,1)} %get-tuple-element.389, s32[]{:T(128)S(6)} %copy.94, bf16[1024,16,80]{0,2,1:T(8,128)(2,1)S(1)} %bitcast.190, bf16[16,512,1024]{2,1,0:T(8,128)(2,1)} %multiply_convert_fusion.10), kind=kOutput, calls=%fused_computation.26.clone.1 | convolution fusion | flops 1342177280 | bytes 22020100 | tf_op jit(solution)/shard_map/while/body/eval_jaxpr/hqk,khe->qhe/dot_general | solution.py:176
  417.2 11.6 %fusion.127 = f32[16,80,1024]{2,1,0:T(8,128)} fusion(bf16[16,512,1024]{2,1,0:T(8,128)(2,1)} %multiply_convert_fusion.10, bf16[2,512,16,80]{1,3,2,0:T(8,128)(2,1)} %copy-done, s32[]{:T(128)S(6)} %copy.94), kind=kOutput, calls=%fused_computation.32.clone.1 | convolution fusion | flops 1342177280 | bytes 23330820 | tf_op jit(solution)/shard_map/while/body/eval_jaxpr/hqk,qhe->khe/dot_general | solution.py:179
  428.8 5.9 copy.70
  434.7 8.8 constant_dynamic-update-slice_fusion.9
  450.2 14.5 %fusion.124 = f32[16,512,1024]{2,1,0:T(8,128)} fusion(bf16[1024,16,80]{0,2,1:T(8,128)(2,1)S(1)} %bitcast.189, bf16[2,512,16,80]{1,3,2,0:T(8,128)(2,1)} %copy-done, s32[]{:T(128)S(6)} %copy.94), kind=kOutput, calls=%fused_computation.34.clone.1 | convolution fusion | flops 1342177280 | bytes 37486596 | tf_op jit(solution)/shard_map/while/body/eval_jaxpr/qhe,khe->hqk/dot_general | solution.py:29
  464.7 17.1 %fusion.126 = f32[16,80,1024]{2,1,0:T(8,128)} fusion(f32[16,512,1024]{2,1,0:T(8,128)} %fusion.124, f32[16,512]{1,0:T(8,128)S(1)} %dynamic-slice_bitcast_fusion.2, pred[512,1024]{1,0:T(8,128)(4,1)S(1)} %fusion.125, bf16[2,512,16,80]{1,3,2,0:T(8,128)(2,1)} %get-tuple-element.409, s32[]{:T(128)S(6)} %copy.94), kind=kOutput, calls=%fused_computation.22.clone.1 | convolution fusion | flops 1367343104 | bytes 40665092 | tf_op jit(solution)/shard_map/while/body/eval_jaxpr/hqk,qhe->khe/dot_general | solution.py:182
  481.8 5.9 copy.69
  487.7 25.4 %multiply_reduce_fusion.5 = (f32[16,512]{1,0:T(8,128)S(1)}, f32[16,512,1024]{2,1,0:T(8,128)}) fusion(f32[16,512,1024]{2,1,0:T(8,128)} %fusion.124, f32[16,512]{1,0:T(8,128)S(1)} %dynamic-slice_bitcast_fusion.2, pred[512,1024]{1,0:T(8,128)(4,1)S(1)} %fusion.125, bf16[1024,16,80]{0,2,1:T(8,128)(2,1)} %bitcast.194, ...), kind=kOutput, calls=%fused_computation.19.clone.1 | convolution fusion | flops 1375723520 | bytes 71630848 | tf_op jit(solution)/shard_map/while/body/eval_jaxpr/qhe,khe->hqk/dot_general | solution.py:171
  513.1 27.9 %multiply_convert_fusion.10 = bf16[16,512,1024]{2,1,0:T(8,128)(2,1)} fusion(f32[16,512,1024]{2,1,0:T(8,128)} %get-tuple-element.345, f32[16,512,1024]{2,1,0:T(8,128)} %fusion.124, f32[16,512]{1,0:T(8,128)S(1)} %get-tuple-element.346, f32[16,512]{1,0:T(8,128)S(1)} %dynamic-slice_bitcast_fusion.2, pred[512,1024]{1,0:T(8,128)(4,1)S(1)} %fusion.125), kind=kLoop, calls=%fused_computation.18.clone.1 | loop fusion | flops 41943040 | bytes 84475904 | tf_op jit(solution)/shard_map/while/body/eval_jaxpr/convert_element_type | solution.py:175
  541.0 12.0 %bitcast_dynamic-update-slice_fusion.8 = bf16[2,512,16,80]{1,3,2,0:T(8,128)(2,1)} fusion(bf16[2,512,16,80]{1,3,2,0:T(8,128)(2,1)} %get-tuple-element.389, s32[]{:T(128)S(6)} %copy.94, bf16[1024,16,80]{0,2,1:T(8,128)(2,1)S(1)} %bitcast.190, bf16[16,512,1024]{2,1,0:T(8,128)(2,1)} %multiply_convert_fusion.10), kind=kOutput, calls=%fused_computation.26.clone.1 | convolution fusion | flops 1342177280 | bytes 22020100 | tf_op jit(solution)/shard_map/while/body/eval_jaxpr/hqk,khe->qhe/dot_general | solution.py:176
  553.0 11.6 %fusion.127 = f32[16,80,1024]{2,1,0:T(8,128)} fusion(bf16[16,512,1024]{2,1,0:T(8,128)(2,1)} %multiply_convert_fusion.10, bf16[2,512,16,80]{1,3,2,0:T(8,128)(2,1)} %copy-done, s32[]{:T(128)S(6)} %copy.94), kind=kOutput, calls=%fused_computation.32.clone.1 | convolution fusion | flops 1342177280 | bytes 23330820 | tf_op jit(solution)/shard_map/while/body/eval_jaxpr/hqk,qhe->khe/dot_general | solution.py:179
  564.6 5.9 copy.70
  570.5 8.8 constant_dynamic-update-slice_fusion.9
  581.5 9.0 convolution_convert_fusion
  590.6 11.4 %convolution_convert_fusion.1 = bf16[1280,1280]{1,0:T(8,128)(2,1)} fusion(bf16[1024,1280]{1,0:T(8,128)(2,1)} %copy-done.47, f32[1024,1280]{1,0:T(8,128)} %get-tuple-element.212, f32[1280]{0:T(1024)S(1)} %copy-done.33, f32[1024]{0:T(1024)S(1)} %copy-done.31), kind=kOutput, calls=%fused_computation.57 | convolution fusion | flops 3361013760 | bytes 11150336 | tf_op jit(solution)/shard_map/nd,nf->df/dot_general | solution.py:151
  602.1 7.4 convolution_convert_fusion.2
  609.8 6.2 fusion.34
  621.1 5.1 convolution_convert_fusion.3
  630.5 5.1 fusion.32
  640.0 5.1 fusion.31
  647.2 8.7 fusion.57
  655.9 7.4 reduce-scatter.23.cloned.1.call-done
  663.2 41.3 %reduce-scatter.21.cloned.1.call-done = bf16[320,1280]{1,0:T(8,128)(2,1)} async-done(((bf16[1280,1280]{1,0:T(8,128)(2,1)}), bf16[320,1280]{1,0:T(8,128)(2,1)}) %reduce-scatter.21.cloned.1.call-update) | async-done | bytes 819216 | tf_op jit(solution)/shard_map/reduce_scatter | solution.py:234
  704.5 41.2 %reduce-scatter.19.cloned.1.call-done = bf16[320,1280]{1,0:T(8,128)(2,1)} async-done(((bf16[1280,1280]{1,0:T(8,128)(2,1)}), bf16[320,1280]{1,0:T(8,128)(2,1)}) %reduce-scatter.19.cloned.1.call-update) | async-done | bytes 819216 | tf_op jit(solution)/shard_map/reduce_scatter | solution.py:231
  745.7 41.3 %reduce-scatter.13.cloned.1.call-done = bf16[320,1280]{1,0:T(8,128)(2,1)} async-done(((bf16[1280,1280]{1,0:T(8,128)(2,1)}), bf16[320,1280]{1,0:T(8,128)(2,1)}) %reduce-scatter.13.cloned.1.call-update) | async-done | bytes 819216 | tf_op jit(solution)/shard_map/reduce_scatter | solution.py:222
  787.0 41.2 %reduce-scatter.17.cloned.1.call-done = bf16[320,1280]{1,0:T(8,128)(2,1)} async-done(((bf16[1280,1280]{1,0:T(8,128)(2,1)}), bf16[320,1280]{1,0:T(8,128)(2,1)}) %reduce-scatter.17.cloned.1.call-update) | async-done | bytes 819216 | tf_op jit(solution)/shard_map/reduce_scatter | solution.py:228
  828.2 41.1 %reduce-scatter.15.cloned.1.call-done = bf16[320,1280]{1,0:T(8,128)(2,1)} async-done(((bf16[1280,1280]{1,0:T(8,128)(2,1)}), bf16[320,1280]{1,0:T(8,128)(2,1)}) %reduce-scatter.15.cloned.1.call-update) | async-done | bytes 819216 | tf_op jit(solution)/shard_map/reduce_scatter | solution.py:225
  869.3 10.7 add_convert_fusion
  880.1 19.9 %all-gather.23.cloned.1.call-done = bf16[1280,1280]{1,0:T(8,128)(2,1)} async-done(((bf16[320,1280]{1,0:T(8,128)(2,1)}), bf16[1280,1280]{1,0:T(8,128)(2,1)}) %all-gather.23.cloned.1.call-update) | async-done | bytes 3276816 | tf_op jit(solution)/shard_map/all_gather | solution.py:134
  900.0 6.4 fusion.58
  906.8 6.3 fusion.46
  913.1 46.6 %all-reduce = (f32[1280]{0:T(1024)}, f32[1280]{0:T(1024)}, f32[1280]{0:T(1024)}, f32[1280]{0:T(1024)}, f32[80]{0:T(128)}) all-reduce(f32[1280]{0:T(1024)S(1)} %copy-done.34, f32[1280]{0:T(1024)S(1)} %convert_reduce_fusion, f32[1280]{0:T(1024)S(1)} %get-tuple-element.144, ...), channel_id=1, replica_groups=mesh['rep'=8,'fsdp'=2,'ctx'=2] {'rep','fsdp','ctx'}, use_global_device_ids=true, to_apply=%region_24.25 | all-reduce | flops 5200 | bytes 41600 | tf_op jit(solution)/shard_map/psum | solution.py:249
  959.7 5.9 fusion.43
  965.5 114.8 %all-reduce.4.cloned.1.call-done = (bf16[320,1280]{1,0:T(8,128)(2,1)}, bf16[320,1280]{1,0:T(8,128)(2,1)}, bf16[320,1280]{1,0:T(8,128)(2,1)}, bf16[320,1280]{1,0:...) async-done(((bf16[320,1280]{1,0:T(8,128)(2,1)}, bf16[320,1280]{1,0:T(8,128)(2,1)}, bf16[320,1280]{1,0:T(8,128)(2,1)}, bf16[320,1280]{1,0:T(8,128)(2,1)}, ...) | async-done | bytes 4915216 | tf_op jit(solution)/shard_map/psum | solution.py:242
  (214 shorter events, 85.3 us)
Async XLA Ops:
  7.2 19.4 %copy-start.8 = (bf16[320,1280]{1,0:T(8,128)(2,1)S(1)}, bf16[320,1280]{1,0:T(8,128)(2,1)}, u32[]{:S(2)}) copy-start(bf16[320,1280]{1,0:T(8,128)(2,1)} %param.21) | copy-start | bytes 2457604
  7.2 18.7 %copy-start.3 = (bf16[2,512,1280]{2,1,0:T(8,128)(2,1)S(1)}, bf16[2,512,1280]{2,1,0:T(8,128)(2,1)}, u32[]{:S(2)}) copy-start(bf16[2,512,1280]{2,1,0:T(8,128)(2,1)} %param.18) | copy-start | bytes 7864324
  7.2 19.4 %copy-start.26 = (f32[1280]{0:T(1024)S(1)}, f32[1280]{0:T(1024)}, u32[]{:S(2)}) copy-start(f32[1280]{0:T(1024)} %param.28) | copy-start | bytes 15364
  7.2 91.6 %all-gather.9.cloned.1.call-start = ((), (), s32[]{:S(2)}) async-start(), calls=%async_computation.8 | async-start | bytes 4096000 | tf_op jit(solution)/shard_map/all_gather | solution.py:77
  7.9 107.6 %all-gather.13.cloned.1.call-start = ((), (), s32[]{:S(2)}) async-start(), calls=%async_computation.10 | async-start | bytes 4096000 | tf_op jit(solution)/shard_map/all_gather | solution.py:75
  8.7 121.4 %all-gather.15.cloned.1.call-start = ((), (), s32[]{:S(2)}) async-start(), calls=%async_computation.11 | async-start | bytes 7864320 | tf_op jit(solution)/shard_map/all_gather | solution.py:101
  8.7 14.5 %collective-permute-start = (bf16[320,1280]{1,0:T(8,128)(2,1)}, bf16[320,1280]{1,0:T(8,128)(2,1)}, u32[]{:S(2)}, u32[]{:S(2)}) collective-permute-start(bf16[320,1280]{1,0:T(8,128)(2,1)} %param.21), channel_id=1, source_target_pairs={{0,3},{1,0},{2,1},{3,2},{4,7},{5,4},{6,5},{7,6},{8,11},{9,8},{10,9... | collective-permute-start | bytes 2457608 | tf_op jit(solution)/shard_map/ppermute | solution.py:62
  25.9 59.1 %collective-permute-start.1 = (bf16[640,1280]{1,0:T(8,128)(2,1)}, bf16[640,1280]{1,0:T(8,128)(2,1)}, u32[]{:S(2)}, u32[]{:S(2)}) collective-permute-start(bf16[640,1280]{1,0:T(8,128)(2,1)} %pad_maximum_fusion), channel_id=1, source_target_pairs={{0,2},{1,3},{2,0},{3,1},{4,6},{5,7},{6,4},{7,5},{8,10},{9,11},{10,... | collective-permute-start | bytes 4915208 | tf_op jit(solution)/shard_map/ppermute | solution.py:62
  26.5 60.0 %copy-start.28 = (f32[1,4,2,128]{3,1,2,0:T(4,128)}, f32[1,4,2,128]{3,1,2,0:T(4,128)S(1)}, u32[]{:S(2)}) copy-start(f32[1,4,2,128]{3,1,2,0:T(4,128)S(1)} %copy.64) | copy-start | bytes 12292
  27.3 62.1 %copy-start.18 = (bf16[1024,1280]{1,0:T(8,128)(2,1)}, bf16[1024,1280]{1,0:T(8,128)(2,1)S(1)}, u32[]{:S(2)}) copy-start(bf16[1024,1280]{1,0:T(8,128)(2,1)S(1)} %fusion.39) | copy-start | bytes 7864324
  98.7 36.1 %all-gather.11.cloned.1.call-start = ((), (), s32[]{:S(2)}) async-start(), calls=%async_computation.9 | async-start | bytes 7864320 | tf_op jit(solution)/shard_map/all_gather | solution.py:102
  106.6 6.8 copy-start.44
  111.2 136.0 %all-gather.17.cloned.1.call-start = ((), (), s32[]{:S(2)}) async-start(), calls=%async_computation.12 | async-start | bytes 4096000 | tf_op jit(solution)/shard_map/all_gather | solution.py:78
  111.8 145.1 %all-gather.19.cloned.1.call-start = ((), (), s32[]{:S(2)}) async-start(), calls=%async_computation.13 | async-start | bytes 4096000 | tf_op jit(solution)/shard_map/all_gather | solution.py:79
  112.3 153.9 %all-gather.21.cloned.1.call-start = ((), (), s32[]{:S(2)}) async-start(), calls=%async_computation.14 | async-start | bytes 4096000 | tf_op jit(solution)/shard_map/all_gather | solution.py:80
  113.1 513.2 %reduce-scatter.11.cloned.1.call-start = ((), (), s32[]{:S(2)}) async-start(), calls=%async_computation.17 | async-start | bytes 15728640 | tf_op jit(solution)/shard_map/reduce_scatter | solution.py:196
  113.4 7.8 copy-start.36
  121.2 15.5 %copy-start.43 = (s32[2]{0:T(128)S(1)}, s32[2]{0:T(128)}, u32[]{:S(2)}) copy-start(s32[2]{0:T(128)} %param.19) | copy-start | bytes 28
  156.4 15.4 %copy-start.5 = (bf16[1,1024,1280]{1,2,0:T(8,128)(2,1)S(1)}, bf16[1,1024,1280]{1,2,0:T(8,128)(2,1)}, u32[]{:S(2)}) copy-start(bf16[1,1024,1280]{1,2,0:T(8,128)(2,1)} %get-tuple-element.330) | copy-start | bytes 7864324 | tf_op jit(solution)/shard_map/while
  156.4 15.4 %copy-start.9 = (bf16[2,512,16,80]{1,3,2,0:T(8,128)(2,1)S(1)}, bf16[2,512,16,80]{1,3,2,0:T(8,128)(2,1)}, u32[]{:S(2)}) copy-start(bf16[2,512,16,80]{1,3,2,0:T(8,128)(2,1)} %get-tuple-element.359) | copy-start | bytes 7864324 | tf_op jit(solution)/shard_map/while
  209.2 15.4 %copy-start.5 = (bf16[1,1024,1280]{1,2,0:T(8,128)(2,1)S(1)}, bf16[1,1024,1280]{1,2,0:T(8,128)(2,1)}, u32[]{:S(2)}) copy-start(bf16[1,1024,1280]{1,2,0:T(8,128)(2,1)} %get-tuple-element.330) | copy-start | bytes 7864324 | tf_op jit(solution)/shard_map/while
  209.2 15.4 %copy-start.9 = (bf16[2,512,16,80]{1,3,2,0:T(8,128)(2,1)S(1)}, bf16[2,512,16,80]{1,3,2,0:T(8,128)(2,1)}, u32[]{:S(2)}) copy-start(bf16[2,512,16,80]{1,3,2,0:T(8,128)(2,1)} %get-tuple-element.359) | copy-start | bytes 7864324 | tf_op jit(solution)/shard_map/while
  247.2 9.7 copy-start.32
  256.9 24.0 %copy-start.30 = (f32[1024]{0:T(1024)}, f32[1024]{0:T(1024)S(1)}, u32[]{:S(2)}) copy-start(f32[1024]{0:T(1024)S(1)} %get-tuple-element.206) | copy-start | bytes 12292
  256.9 9.4 copy-start.41
  266.3 10.1 copy-start.7
  266.3 10.1 copy-start.39
  276.3 4.5 copy-start.47
  276.3 4.5 copy-start.12
  280.9 4.3 copy-start.15
  282.7 2.4 copy-start.6
  307.7 6.4 copy-start
  307.7 6.4 copy-start.2
  434.7 8.8 copy-start.1
  443.5 6.4 copy-start
  443.5 6.4 copy-start.2
  570.5 8.8 copy-start.1
  579.7 56.0 %reduce-scatter.9.cloned.1.call-start = ((), (), s32[]{:S(2)}) async-start(), calls=%async_computation.15 | async-start | bytes 15728640 | tf_op jit(solution)/shard_map/reduce_scatter | solution.py:195
  580.5 10.1 copy-start.31
  580.5 10.1 copy-start.33
  580.5 82.7 %reduce-scatter.23.cloned.1.call-start = ((), (), s32[]{:S(2)}) async-start(), calls=%async_computation.23 | async-start | bytes 4096000 | tf_op jit(solution)/shard_map/reduce_scatter | solution.py:237
  590.5 11.6 %copy-start.11 = (bf16[160,8,2,512]{3,1,2,0:T(8,128)(2,1)S(1)}, bf16[160,8,2,512]{3,1,2,0:T(8,128)(2,1)}, u32[]{:S(2)}) copy-start(bf16[160,8,2,512]{3,1,2,0:T(8,128)(2,1)} %copy.65) | copy-start | bytes 7864324
  590.6 114.0 %reduce-scatter.21.cloned.1.call-start = ((), (), s32[]{:S(2)}) async-start(), calls=%async_computation.22 | async-start | bytes 4096000 | tf_op jit(solution)/shard_map/reduce_scatter | solution.py:234
  602.1 7.7 copy-start.37
  602.1 143.6 %reduce-scatter.19.cloned.1.call-start = ((), (), s32[]{:S(2)}) async-start(), calls=%async_computation.21 | async-start | bytes 4096000 | tf_op jit(solution)/shard_map/reduce_scatter | solution.py:231
  609.6 177.4 %reduce-scatter.13.cloned.1.call-start = ((), (), s32[]{:S(2)}) async-start(), calls=%async_computation.18 | async-start | bytes 4096000 | tf_op jit(solution)/shard_map/reduce_scatter | solution.py:222
  616.0 5.0 copy-start.17
  626.2 202.0 %reduce-scatter.17.cloned.1.call-start = ((), (), s32[]{:S(2)}) async-start(), calls=%async_computation.20 | async-start | bytes 4096000 | tf_op jit(solution)/shard_map/reduce_scatter | solution.py:228
  635.7 233.7 %reduce-scatter.15.cloned.1.call-start = ((), (), s32[]{:S(2)}) async-start(), calls=%async_computation.19 | async-start | bytes 4096000 | tf_op jit(solution)/shard_map/reduce_scatter | solution.py:225
  640.0 5.9 copy-start.29
  645.0 255.0 %all-gather.23.cloned.1.call-start = ((), (), s32[]{:S(2)}) async-start(), calls=%async_computation.16 | async-start | bytes 4096000 | tf_op jit(solution)/shard_map/all_gather | solution.py:134
  645.6 434.7 %all-reduce.4.cloned.1.call-start = ((), (), s32[]{:S(2)}) async-start(), calls=%async_computation.24 | async-start | bytes 9830400 | tf_op jit(solution)/shard_map/psum | solution.py:242
  647.2 222.1 %copy-start.40 = (f32[1280]{0:T(1024)S(1)}, f32[1280]{0:T(1024)}, u32[]{:S(2)}) copy-start(f32[1280]{0:T(1024)} %param.27) | copy-start | bytes 15364
  900.0 6.5 copy-start.4
  900.0 6.5 copy-start.20
  900.0 6.5 copy-start.27
  900.0 6.5 copy-start.38
  900.0 6.7 copy-start.46
  906.8 6.3 copy-start.34
  906.8 6.3 copy-start.35
  1080.3 5.1 copy-start.25
  1080.3 6.3 copy-start.24
  1080.3 7.6 copy-start.23
  1082.9 6.3 copy-start.22
  (9 other events, 15.0 us)
Sparse Core Ops, SparseCore 0:
  9.6 42.6 all-gather.8
  53.8 40.4 all-gather.12
  98.8 17.5 all-gather.14
  118.4 16.3 all-gather.10
  136.2 30.4 all-gather.16
  168.1 29.2 all-gather.18
  199.0 29.2 all-gather.20
  579.9 19.2 reduce-scatter.10
  601.5 19.2 reduce-scatter.8
  623.2 39.9 reduce-scatter.22
  665.8 38.6 reduce-scatter.20
  707.0 38.6 reduce-scatter.18
  748.3 38.6 reduce-scatter.12
  789.4 38.6 reduce-scatter.16
  830.6 38.6 reduce-scatter.14
  870.7 29.2 all-gather.22
  904.2 176.0 all-reduce.3
